TPU v7x, 32 devices: a whole 2x2x4 slice. The times are simulated.
32 devices in a mesh: conv: 2 (over y), ctx: 4 (over x, core), head: 4 (over z).
Axes of the slice: x: 2, y: 2, z: 4, core: 2. Of those that a mesh axis runs over, the one named last changes fastest.
Arguments:
- queries: bfloat16 [512, 64, 128], P(('conv', 'ctx'), 'head'), parts along dimension 0, may hold values from -240 to 240, as said below
- new_keys: bfloat16 [512, 8, 128], P(('conv', 'ctx'), 'head'), parts along dimension 0, may hold values from -8 to 8
- new_values: bfloat16 [512, 8, 128], P(('conv', 'ctx'), 'head'), parts along dimension 0, may hold values from -18 to 18
- cache_keys: bfloat16 [16384, 8, 128], P(('conv', 'ctx'), 'head'), parts along dimension 0, may hold values from -6 to 6
- cache_values: bfloat16 [16384, 8, 128], P(('conv', 'ctx'), 'head'), parts along dimension 0, may hold values from -18 to 18
- cache_len: int32 [2], P('conv'), parts along dimension 0, may hold values from 4097 to 8192
Outputs:
- attended: bfloat16 [512, 64, 128], P(('conv', 'ctx'), 'head'), parts along dimension 0
There are 2 independent parts, one for each index of `conv`. A program takes and returns all parts, laid end to end along the dimension named above; each array names one. Nothing has to cross between parts.
Inputs may be any that keep to these rules, and one draw needn't show every extreme that they name: `queries`: each query row is a row of independent entries times a row scale.
All inputs are finite; a program needn't handle non-finite values.
Results may differ from a plain program's by a relative error of at most 0.01.
Values may be sent and summed in bfloat16 or wider, within the bound.
A program may use at most 64 MiB of HBM per device.

v0:
```python
import math

import jax
import jax.numpy as jnp
from jax import lax
from jax.sharding import PartitionSpec as P

NEG_FILL = -1e30


def attend_block(query_rows, keys, values, valid):
    scores = jnp.einsum("tkgd,skd->tkgs", query_rows, keys, preferred_element_type=jnp.float32) * (
        1.0 / math.sqrt(keys.shape[-1])
    )
    mask = valid[:, None, None, :]
    scores = jnp.where(mask, scores, NEG_FILL)
    peak = jnp.max(scores, axis=-1)
    expo = jnp.where(mask, jnp.exp(scores - peak[..., None]), 0.0)
    total = jnp.sum(expo, axis=-1)
    out = jnp.einsum(
        "tkgs,skd->tkgd", expo.astype(jnp.bfloat16), values, preferred_element_type=jnp.float32
    )
    return (out, peak, total)


def per_device(queries, new_keys, new_values, cache_keys, cache_values, cache_len):
    q_rows, heads_local, head_size = queries.shape
    slots, kv_local, _ = cache_keys.shape
    group = heads_local // kv_local
    place = lax.axis_index("ctx")
    limit = cache_len[0]
    slot_valid = place * slots + lax.iota(jnp.int32, slots) < limit
    piece = lax.all_gather(queries, "ctx", axis=0, tiled=True)
    rows = piece.shape[0]
    block = math.gcd(rows, 64)
    blocks = piece.reshape(rows // block, block, kv_local, group, head_size)

    def one_block(blk):
        out, peak, total = attend_block(blk, cache_keys, cache_values, slot_valid[None, :])
        floored = jnp.maximum(total, 1.0)
        norm = (out / floored[..., None]).astype(jnp.bfloat16)
        lse = peak + jnp.log(floored)
        return (norm.reshape(block, heads_local, head_size), lse.reshape(block, heads_local))

    norm, lse = lax.map(one_block, blocks)
    norm, lse = (norm.reshape(rows, heads_local, head_size), lse.reshape(rows, heads_local))
    turn_k, turn_v = (
        lax.all_gather(new_keys, "ctx", axis=0, tiled=True),
        lax.all_gather(new_values, "ctx", axis=0, tiled=True),
    )
    own_ids = place * q_rows + lax.iota(jnp.int32, q_rows)
    causal = lax.iota(jnp.int32, turn_k.shape[0])[None, :] <= own_ids[:, None]
    turn_out, turn_max, turn_total = attend_block(
        queries.reshape(q_rows, kv_local, group, head_size), turn_k, turn_v, causal
    )
    turn_out = turn_out.reshape(q_rows, heads_local, head_size)
    turn_max = turn_max.reshape(q_rows, heads_local)
    turn_total = turn_total.reshape(q_rows, heads_local)
    got_norm = lax.all_to_all(norm[None], "ctx", split_axis=1, concat_axis=0, tiled=True)
    got_lse = lax.all_to_all(lse[None], "ctx", split_axis=1, concat_axis=0, tiled=True)
    top = jnp.maximum(jnp.max(got_lse, axis=0), turn_max)
    shard_scale = jnp.exp(got_lse - top[None])
    numer = jnp.einsum("sthd,sth->thd", got_norm.astype(jnp.float32), shard_scale)
    denom = jnp.sum(shard_scale, axis=0)
    turn_scale = jnp.exp(turn_max - top)
    numer = numer + turn_out * turn_scale[..., None]
    denom = denom + turn_total * turn_scale
    return (numer / denom[..., None]).astype(jnp.bfloat16)


def solution(mesh):
    return jax.shard_map(
        per_device,
        mesh=mesh,
        in_specs=(
            P(("conv", "ctx"), "head", None),
            P(("conv", "ctx"), "head", None),
            P(("conv", "ctx"), "head", None),
            P(("conv", "ctx"), "head", None),
            P(("conv", "ctx"), "head", None),
            P("conv"),
        ),
        out_specs=P(("conv", "ctx"), "head", None),
        check_vma=False,
    )
```

profile of v0, /device:TPU:0, one launch (start us, length us, event | category | flops | bytes accessed | tf_op | source)
XLA Modules:
  0.0 124.3 jit_solution(1532145493059581780)
XLA Ops:
  11.5 6.5 %all_gather.10 = bf16[256,2,128]{2,0,1:T(8,128)(2,1)S(1)} all-gather(bf16[64,2,128]{2,0,1:T(8,128)(2,1)S(1)} %copy.100), channel_id=1, replica_groups=mesh['conv'=2,'ctx'=4,'head'=4] {'ctx'}, dimensions={0}, use_global_device_ids=true | all-gather | bytes 163840 | tf_op jit(solution)/shard_map/all_gather | solution.py:48
  18.0 6.3 %all_gather.11 = bf16[256,2,128]{2,0,1:T(8,128)(2,1)S(1)} all-gather(bf16[64,2,128]{2,0,1:T(8,128)(2,1)S(1)} %copy.104), channel_id=1, replica_groups=mesh['conv'=2,'ctx'=4,'head'=4] {'ctx'}, dimensions={0}, use_global_device_ids=true | all-gather | bytes 163840 | tf_op jit(solution)/shard_map/all_gather | solution.py:49
  26.2 2.8 %all-gather.2.cloned.1.call-done = bf16[256,16,128]{2,1,0:T(8,128)(2,1)} async-done(((bf16[64,16,128]{2,1,0:T(8,128)(2,1)}), bf16[256,16,128]{2,1,0:T(8,128)(2,1)}) %all-gather.2.cloned.1.call-update) | async-done | bytes 1048592 | tf_op jit(solution)/shard_map/all_gather | solution.py:33
  29.0 58.6 %while.13 = (s32[]{:T(128)}, bf16[4,64,16,128]{3,2,1,0:T(8,128)(2,1)}, f32[4,64,16]{1,2,0:T(8,128)S(1)}, bf16[4,64,2,8,128]{4,3,2,1,0:T(8,128)(2,1)}, bf16[2048,...) while((s32[]{:T(128)}, ...), condition=%wide.region_3.4_spmd.clone, body=%wide.region_0.3_spmd.clone.sunk | while | flops 1101272064 | bytes 61953156 | solution.py:45
  29.7 2.4 %bitcast_reduce_fusion.2 = (f32[64,2,8]{2,0,1:T(8,128)S(1)}, f32[2,64,8,2048]{3,2,1,0:T(8,128)S(1)}) fusion(pred[2048]{0:T(1024)(128)(4,1)S(1)} %add_compare_fusion.2, bf16[2048,2,128]{2,0,1:T(8,128)(2,1)S(1)} %get-tuple-element.220, bf16[4,64,2,8,128]{4,3,2,1,0:T(8,128)(2,1)} %get-tuple-element.219, s32[]{:T(128)} %get-tuple-element.207), kind=kOutput, calls=%fused_computation.2.clone.1 | convolution fusion | flops 543161344 | bytes 9705984 | tf_op jit(solution)/shard_map/while/body/eval_jaxpr/tkgd,skd->tkgs/dot_general | solution.py:12
  32.1 3.2 %copy-done = f32[2,64,8,2048]{3,2,1,0:T(8,128)} copy-done((f32[2,64,8,2048]{3,2,1,0:T(8,128)}, f32[2,64,8,2048]{3,2,1,0:T(8,128)S(1)}, u32[]{:S(2)}) %copy-start) | copy-done | bytes 8388632 | tf_op jit(solution)/shard_map/while
  35.4 2.2 %fusion.55 = f32[64,2,8]{2,0,1:T(8,128)S(1)} fusion(f32[2,64,8,2048]{3,2,1,0:T(8,128)S(1)} %get-tuple-element.196, f32[64,2,8]{2,0,1:T(8,128)S(1)} %get-tuple-element.197, pred[2048]{0:T(1024)(128)(4,1)S(1)} %add_compare_fusion.2), kind=kLoop, calls=%fused_computation.6.clone.1 | loop fusion | flops 10484736 | bytes 8398848 | tf_op jit(solution)/shard_map/while/body/eval_jaxpr/reduce_sum | solution.py:19
  37.8 5.1 %fusion.56 = bf16[64,2,8,128]{3,2,0,1:T(8,128)(2,1)S(1)} fusion(bf16[2048,2,128]{2,0,1:T(8,128)(2,1)S(1)} %get-tuple-element.221, f32[2,64,8,2048]{3,2,1,0:T(8,128)} %copy-done, f32[64,2,8]{2,0,1:T(8,128)S(1)} %get-tuple-element.197, pred[2048]{0:T(1024)(128)(4,1)S(1)} %add_compare_fusion.2, f32[64,2,8]{2,0,1:T(8,128)S(1)} %copy.142), kind=kOutput, calls=%fused_computation.16.clone.1 | convolution fusion | flops 547618816 | bytes 9709568 | tf_op jit(solution)/shard_map/while/body/eval_jaxpr/tkgs,skd->tkgd/dot_general | solution.py:20
  44.3 2.4 %bitcast_reduce_fusion.2 = (f32[64,2,8]{2,0,1:T(8,128)S(1)}, f32[2,64,8,2048]{3,2,1,0:T(8,128)S(1)}) fusion(pred[2048]{0:T(1024)(128)(4,1)S(1)} %add_compare_fusion.2, bf16[2048,2,128]{2,0,1:T(8,128)(2,1)S(1)} %get-tuple-element.220, bf16[4,64,2,8,128]{4,3,2,1,0:T(8,128)(2,1)} %get-tuple-element.219, s32[]{:T(128)} %get-tuple-element.207), kind=kOutput, calls=%fused_computation.2.clone.1 | convolution fusion | flops 543161344 | bytes 9705984 | tf_op jit(solution)/shard_map/while/body/eval_jaxpr/tkgd,skd->tkgs/dot_general | solution.py:12
  46.8 3.2 %copy-done = f32[2,64,8,2048]{3,2,1,0:T(8,128)} copy-done((f32[2,64,8,2048]{3,2,1,0:T(8,128)}, f32[2,64,8,2048]{3,2,1,0:T(8,128)S(1)}, u32[]{:S(2)}) %copy-start) | copy-done | bytes 8388632 | tf_op jit(solution)/shard_map/while
  50.0 2.2 %fusion.55 = f32[64,2,8]{2,0,1:T(8,128)S(1)} fusion(f32[2,64,8,2048]{3,2,1,0:T(8,128)S(1)} %get-tuple-element.196, f32[64,2,8]{2,0,1:T(8,128)S(1)} %get-tuple-element.197, pred[2048]{0:T(1024)(128)(4,1)S(1)} %add_compare_fusion.2), kind=kLoop, calls=%fused_computation.6.clone.1 | loop fusion | flops 10484736 | bytes 8398848 | tf_op jit(solution)/shard_map/while/body/eval_jaxpr/reduce_sum | solution.py:19
  52.5 5.1 %fusion.56 = bf16[64,2,8,128]{3,2,0,1:T(8,128)(2,1)S(1)} fusion(bf16[2048,2,128]{2,0,1:T(8,128)(2,1)S(1)} %get-tuple-element.221, f32[2,64,8,2048]{3,2,1,0:T(8,128)} %copy-done, f32[64,2,8]{2,0,1:T(8,128)S(1)} %get-tuple-element.197, pred[2048]{0:T(1024)(128)(4,1)S(1)} %add_compare_fusion.2, f32[64,2,8]{2,0,1:T(8,128)S(1)} %copy.142), kind=kOutput, calls=%fused_computation.16.clone.1 | convolution fusion | flops 547618816 | bytes 9709568 | tf_op jit(solution)/shard_map/while/body/eval_jaxpr/tkgs,skd->tkgd/dot_general | solution.py:20
  59.0 2.4 %bitcast_reduce_fusion.2 = (f32[64,2,8]{2,0,1:T(8,128)S(1)}, f32[2,64,8,2048]{3,2,1,0:T(8,128)S(1)}) fusion(pred[2048]{0:T(1024)(128)(4,1)S(1)} %add_compare_fusion.2, bf16[2048,2,128]{2,0,1:T(8,128)(2,1)S(1)} %get-tuple-element.220, bf16[4,64,2,8,128]{4,3,2,1,0:T(8,128)(2,1)} %get-tuple-element.219, s32[]{:T(128)} %get-tuple-element.207), kind=kOutput, calls=%fused_computation.2.clone.1 | convolution fusion | flops 543161344 | bytes 9705984 | tf_op jit(solution)/shard_map/while/body/eval_jaxpr/tkgd,skd->tkgs/dot_general | solution.py:12
  61.4 3.2 %copy-done = f32[2,64,8,2048]{3,2,1,0:T(8,128)} copy-done((f32[2,64,8,2048]{3,2,1,0:T(8,128)}, f32[2,64,8,2048]{3,2,1,0:T(8,128)S(1)}, u32[]{:S(2)}) %copy-start) | copy-done | bytes 8388632 | tf_op jit(solution)/shard_map/while
  64.7 2.2 %fusion.55 = f32[64,2,8]{2,0,1:T(8,128)S(1)} fusion(f32[2,64,8,2048]{3,2,1,0:T(8,128)S(1)} %get-tuple-element.196, f32[64,2,8]{2,0,1:T(8,128)S(1)} %get-tuple-element.197, pred[2048]{0:T(1024)(128)(4,1)S(1)} %add_compare_fusion.2), kind=kLoop, calls=%fused_computation.6.clone.1 | loop fusion | flops 10484736 | bytes 8398848 | tf_op jit(solution)/shard_map/while/body/eval_jaxpr/reduce_sum | solution.py:19
  67.1 5.1 %fusion.56 = bf16[64,2,8,128]{3,2,0,1:T(8,128)(2,1)S(1)} fusion(bf16[2048,2,128]{2,0,1:T(8,128)(2,1)S(1)} %get-tuple-element.221, f32[2,64,8,2048]{3,2,1,0:T(8,128)} %copy-done, f32[64,2,8]{2,0,1:T(8,128)S(1)} %get-tuple-element.197, pred[2048]{0:T(1024)(128)(4,1)S(1)} %add_compare_fusion.2, f32[64,2,8]{2,0,1:T(8,128)S(1)} %copy.142), kind=kOutput, calls=%fused_computation.16.clone.1 | convolution fusion | flops 547618816 | bytes 9709568 | tf_op jit(solution)/shard_map/while/body/eval_jaxpr/tkgs,skd->tkgd/dot_general | solution.py:20
  73.7 2.4 %bitcast_reduce_fusion.2 = (f32[64,2,8]{2,0,1:T(8,128)S(1)}, f32[2,64,8,2048]{3,2,1,0:T(8,128)S(1)}) fusion(pred[2048]{0:T(1024)(128)(4,1)S(1)} %add_compare_fusion.2, bf16[2048,2,128]{2,0,1:T(8,128)(2,1)S(1)} %get-tuple-element.220, bf16[4,64,2,8,128]{4,3,2,1,0:T(8,128)(2,1)} %get-tuple-element.219, s32[]{:T(128)} %get-tuple-element.207), kind=kOutput, calls=%fused_computation.2.clone.1 | convolution fusion | flops 543161344 | bytes 9705984 | tf_op jit(solution)/shard_map/while/body/eval_jaxpr/tkgd,skd->tkgs/dot_general | solution.py:12
  76.1 3.2 %copy-done = f32[2,64,8,2048]{3,2,1,0:T(8,128)} copy-done((f32[2,64,8,2048]{3,2,1,0:T(8,128)}, f32[2,64,8,2048]{3,2,1,0:T(8,128)S(1)}, u32[]{:S(2)}) %copy-start) | copy-done | bytes 8388632 | tf_op jit(solution)/shard_map/while
  79.3 2.2 %fusion.55 = f32[64,2,8]{2,0,1:T(8,128)S(1)} fusion(f32[2,64,8,2048]{3,2,1,0:T(8,128)S(1)} %get-tuple-element.196, f32[64,2,8]{2,0,1:T(8,128)S(1)} %get-tuple-element.197, pred[2048]{0:T(1024)(128)(4,1)S(1)} %add_compare_fusion.2), kind=kLoop, calls=%fused_computation.6.clone.1 | loop fusion | flops 10484736 | bytes 8398848 | tf_op jit(solution)/shard_map/while/body/eval_jaxpr/reduce_sum | solution.py:19
  81.8 5.1 %fusion.56 = bf16[64,2,8,128]{3,2,0,1:T(8,128)(2,1)S(1)} fusion(bf16[2048,2,128]{2,0,1:T(8,128)(2,1)S(1)} %get-tuple-element.221, f32[2,64,8,2048]{3,2,1,0:T(8,128)} %copy-done, f32[64,2,8]{2,0,1:T(8,128)S(1)} %get-tuple-element.197, pred[2048]{0:T(1024)(128)(4,1)S(1)} %add_compare_fusion.2, f32[64,2,8]{2,0,1:T(8,128)S(1)} %copy.142), kind=kOutput, calls=%fused_computation.16.clone.1 | convolution fusion | flops 547618816 | bytes 9709568 | tf_op jit(solution)/shard_map/while/body/eval_jaxpr/tkgs,skd->tkgd/dot_general | solution.py:20
  90.1 3.3 %all-to-all-start.1 = ((f32[4,1,1024]{2,1,0:T(1,128)}), f32[4,1,1024]{2,1,0:T(1,128)S(1)}, u32[]{:S(2)}, u32[]{:S(2)}) async-start(f32[4,1,1024]{2,1,0:T(1,128)} %reshape.128), calls=%async_computation.1 | async-start | bytes 32768 | tf_op jit(solution)/shard_map/all_to_all | solution.py:60
  93.8 3.4 %all-to-all-done.1 = f32[4,1,1024]{2,1,0:T(1,128)S(1)} async-done(((f32[4,1,1024]{2,1,0:T(1,128)}), f32[4,1,1024]{2,1,0:T(1,128)S(1)}, u32[]{:S(2)}, u32[]{:S(2)}) %all-to-all-start.1) | async-done | bytes 16416 | tf_op jit(solution)/shard_map/all_to_all | solution.py:60
  97.2 3.5 %all-to-all-start = ((bf16[1,256,16,128]{3,2,0,1:T(8,128)(2,1)}), bf16[1,256,16,128]{3,2,0,1:T(8,128)(2,1)S(1)}, u32[]{:S(2)}, u32[]{:S(2)}) async-start(bf16[1,256,16,128]{3,2,0,1:T(8,128)(2,1)} %bitcast.2), calls=%async_computation | async-start | bytes 2097152 | tf_op jit(solution)/shard_map/all_to_all | solution.py:59
  102.9 12.2 %all-to-all-done = bf16[1,256,16,128]{3,2,0,1:T(8,128)(2,1)S(1)} async-done(((bf16[1,256,16,128]{3,2,0,1:T(8,128)(2,1)}), bf16[1,256,16,128]{3,2,0,1:T(8,128)(2,1)S(1)}, u32[]{:S(2)}, u32[]{:S(2)}) %all-to-all-start) | async-done | bytes 1048608 | tf_op jit(solution)/shard_map/all_to_all | solution.py:59
  (64 shorter events, 20.8 us)
Async XLA Ops:
  6.5 22.5 %all-gather.2.cloned.1.call-start = ((), (), s32[]{:S(2)}) async-start(), calls=%async_computation.2 | async-start | bytes 1310720 | tf_op jit(solution)/shard_map/all_gather | solution.py:33
  32.1 3.2 %copy-start = (f32[2,64,8,2048]{3,2,1,0:T(8,128)}, f32[2,64,8,2048]{3,2,1,0:T(8,128)S(1)}, u32[]{:S(2)}) copy-start(f32[2,64,8,2048]{3,2,1,0:T(8,128)S(1)} %get-tuple-element.196) | copy-start | bytes 25165828 | tf_op jit(solution)/shard_map/while
  46.8 3.2 %copy-start = (f32[2,64,8,2048]{3,2,1,0:T(8,128)}, f32[2,64,8,2048]{3,2,1,0:T(8,128)S(1)}, u32[]{:S(2)}) copy-start(f32[2,64,8,2048]{3,2,1,0:T(8,128)S(1)} %get-tuple-element.196) | copy-start | bytes 25165828 | tf_op jit(solution)/shard_map/while
  61.4 3.2 %copy-start = (f32[2,64,8,2048]{3,2,1,0:T(8,128)}, f32[2,64,8,2048]{3,2,1,0:T(8,128)S(1)}, u32[]{:S(2)}) copy-start(f32[2,64,8,2048]{3,2,1,0:T(8,128)S(1)} %get-tuple-element.196) | copy-start | bytes 25165828 | tf_op jit(solution)/shard_map/while
  76.1 3.2 %copy-start = (f32[2,64,8,2048]{3,2,1,0:T(8,128)}, f32[2,64,8,2048]{3,2,1,0:T(8,128)S(1)}, u32[]{:S(2)}) copy-start(f32[2,64,8,2048]{3,2,1,0:T(8,128)S(1)} %get-tuple-element.196) | copy-start | bytes 25165828 | tf_op jit(solution)/shard_map/while
  90.1 7.1 %all-to-all-start.1 = ((f32[4,1,1024]{2,1,0:T(1,128)}), f32[4,1,1024]{2,1,0:T(1,128)S(1)}, u32[]{:S(2)}, u32[]{:S(2)}) async-start(f32[4,1,1024]{2,1,0:T(1,128)} %reshape.128), calls=%async_computation.1 | async-start | bytes 32768 | tf_op jit(solution)/shard_map/all_to_all | solution.py:60
  97.2 17.9 %all-to-all-start = ((bf16[1,256,16,128]{3,2,0,1:T(8,128)(2,1)}), bf16[1,256,16,128]{3,2,0,1:T(8,128)(2,1)S(1)}, u32[]{:S(2)}, u32[]{:S(2)}) async-start(bf16[1,256,16,128]{3,2,0,1:T(8,128)(2,1)} %bitcast.2), calls=%async_computation | async-start | bytes 2097152 | tf_op jit(solution)/shard_map/all_to_all | solution.py:59
Sparse Core Ops, SparseCore 0:
  8.9 20.1 all-gather.1
where the time goes:
time: 125 us; the launch traced here: 124 us
  matrix products  33.2 us (27%)
  local copies, waits for them, and re-layouts  23.8 us (19%)
  waiting for transfers between devices  19.2 us (15%)
  other arithmetic  14.9 us (12%)
  between operations  13.5 us (11%)
  blocking collectives  12.8 us (10%)
  starting transfers between devices  6.77 us (5%)
    dot_general x5, matrix products, attend_block(): jnp.einsum('tkgs,skd->tkgd', expo.astype(jnp.bfloat16), values, preferred...  20.8 us
    while x8, local copies, waits for them, and re-layouts  12.9 us
    all_to_all x1, waiting for transfers between devices, per_device(): lax.all_to_all(norm[None], 'ctx', split_axis=1, concat_axis=0, tiled=True)  12.2 us
    dot_general x5, matrix products, attend_block(): jnp.einsum('tkgd,skd->tkgs', query_rows, keys, preferred_element_type=jnp...  11 us
    reduce_sum x5, other arithmetic, attend_block(): total = jnp.sum(expo, axis=-1)  9.28 us
    all_gather x1, blocking collectives, per_device(): lax.all_gather(new_keys, 'ctx', axis=0, tiled=True)  6.49 us
    all_gather x1, blocking collectives, per_device(): lax.all_gather(new_values, 'ctx', axis=0, tiled=True)  6.3 us
    unnamed x7, local copies, waits for them, and re-layouts  5.81 us
  transfers between devices with their start and end apart: 3, of which 3 were waited for; matrix products, arithmetic and copies ran while one was open for 7% of the time, Pallas kernels for 0%

commit v1 on v0

v1 whole, which is shorter than its diff:
```python
import functools
import math

import jax
import jax.numpy as jnp
from jax import lax
from jax.experimental import pallas as pl
from jax.experimental.pallas import tpu as pltpu
from jax.sharding import PartitionSpec as P

MESH = pl.DeviceIdType.MESH
NEG = -1e30
CHUNK = 256


def column_to_rows(col):
    rows = col.shape[0]
    return [col[i : i + 128].T[0:1, :] for i in range(0, rows, 128)]


def rows_to_column(row):
    return jnp.broadcast_to(row, (128, 128)).T


def kernel(
    chips, nh, group, sub,
    len_ref, q_hbm, nk_ref, nv_ref, k_hbm, v_hbm,
    out_ref,
    k_in, v_in, split, k_s, v_s, dist, q_own, q_part, q_rem, q_rel,
    own_o, own_l, a_o, a_l,
    sp_o, sp_l, sb_o, sb_l, sr_o, sr_l,
    pp_o, pp_l, pb_o, pb_l, pr_o, pr_l,
    loc_sem, send_sem, recv_sem,
):
    tokens, heads, hd = q_hbm.shape
    slots = k_hbm.shape[0] // nh
    rows = tokens * group
    ext = k_s.shape[1] - slots
    me = lax.axis_index("ctx")
    core = lax.rem(me, 2)
    chip = me // 2
    partner = me + 1 - 2 * core
    far = [lax.rem(chip + d, chips) * 2 + core for d in range(1, chips)]
    counter = iter(range(send_sem.shape[0]))

    def remote(src, dst, dev):
        i = next(counter)
        return pltpu.make_async_remote_copy(
            src_ref=src, dst_ref=dst, send_sem=send_sem.at[i], recv_sem=recv_sem.at[i],
            device_id={"ctx": dev}, device_id_type=MESH,
        )

    loads = [
        pltpu.make_async_copy(k_hbm, k_in, loc_sem.at[0]),
        pltpu.make_async_copy(v_hbm, v_in, loc_sem.at[1]),
        pltpu.make_async_copy(q_hbm, q_own, loc_sem.at[2]),
    ]
    for load in loads:
        load.start()

    barrier = pltpu.get_barrier_semaphore()
    for dev in [partner] + far:
        pl.semaphore_signal(barrier, inc=1, device_id={"ctx": dev}, device_id_type=MESH)
    pl.semaphore_wait(barrier, chips)

    send_q_far = [remote(q_hbm, q_rem.at[d], far[d]) for d in range(chips - 1)]
    send_q_part = remote(q_hbm, q_part, partner)
    send_q_rel = [remote(q_rem.at[d], q_rel.at[d], partner) for d in range(chips - 1)]
    send_pp = [
        (remote(sp_o.at[h], pp_o.at[h], partner), remote(sp_l.at[h], pp_l.at[h], partner))
        for h in range(nh)
    ]
    send_pb = [
        [
            (
                remote(sb_o.at[d, h], pb_o.at[d, h], partner),
                remote(sb_l.at[d, h], pb_l.at[d, h], partner),
            )
            for h in range(nh)
        ]
        for d in range(chips - 1)
    ]
    back = [lax.rem(chip + chips - 1 - d, chips) * 2 + core for d in range(chips - 1)]
    send_pr = [
        [
            (
                remote(sr_o.at[d, h], pr_o.at[d, h], back[d]),
                remote(sr_l.at[d, h], pr_l.at[d, h], back[d]),
            )
            for h in range(nh)
        ]
        for d in range(chips - 1)
    ]
    for c in send_q_far:
        c.start()
    send_q_part.start()

    limit = len_ref[0]
    first_slot = me * slots
    filled = first_slot < limit
    loads[0].wait()
    loads[1].wait()
    nk = nk_ref[...].astype(jnp.float32)
    nv = nv_ref[...].astype(jnp.float32)
    k_top = k_in[0:16, :].astype(jnp.float32)
    fill = [jnp.where(filled, k_top[h : h + 1], nk[h : h + 1]) for h in range(nh)]

    def prep(i, _):
        at = pl.multiple_of(i * CHUNK, CHUNK)
        src = pl.ds(pl.multiple_of(i * CHUNK * nh, CHUNK * nh), CHUNK * nh)
        split[0] = k_in[src, :].astype(jnp.float32)
        split[1] = v_in[src, :].astype(jnp.float32)
        ids = first_slot + at + lax.broadcasted_iota(jnp.int32, (CHUNK, hd), 0)
        valid = ids < limit
        ones = jnp.where(valid, 1.0, 0.0).astype(jnp.bfloat16)
        for h in range(nh):
            kh = split[0, pl.ds(h, CHUNK, stride=nh), :]
            vh = split[1, pl.ds(h, CHUNK, stride=nh), :]
            kb = jnp.where(valid, kh, fill[h]).astype(jnp.bfloat16)
            k_s[h, pl.ds(at, CHUNK), 0:hd] = kb
            k_s[h, pl.ds(at, CHUNK), hd : 2 * hd] = kb
            v_s[h, pl.ds(at, CHUNK), 0:hd] = jnp.where(valid, vh, 0.0).astype(jnp.bfloat16)
            v_s[h, pl.ds(at, CHUNK), hd : 2 * hd] = ones
        return 0

    lax.fori_loop(0, slots // CHUNK, prep, 0)
    split[0, 0 : tokens * nh] = nk
    split[1, 0 : tokens * nh] = nv
    for h in range(nh):
        kb = split[0, pl.ds(h, tokens, stride=nh), :].astype(jnp.bfloat16)
        vb = split[1, pl.ds(h, tokens, stride=nh), :].astype(jnp.bfloat16)
        k_s[h, slots : slots + tokens, 0:hd] = kb
        k_s[h, slots : slots + tokens, hd : 2 * hd] = kb
        v_s[h, slots : slots + tokens, 0:hd] = vb
        v_s[h, slots : slots + tokens, hd : 2 * hd] = jnp.ones((tokens, hd), jnp.bfloat16)
        if ext > tokens:
            rest = jnp.zeros((ext - tokens, 2 * hd), jnp.bfloat16)
            k_s[h, slots + tokens :, :] = rest
            v_s[h, slots + tokens :, :] = rest
    row_id = lax.broadcasted_iota(jnp.int32, (rows, ext), 0) // group
    col_id = lax.broadcasted_iota(jnp.int32, (rows, ext), 1)
    dist[...] = jnp.where(col_id < tokens, row_id - col_id, -(2**30))

    scale = math.log2(math.e) / math.sqrt(hd)

    def attend(q_ref, h, block, emit):
        least = (me - block) * tokens
        some = jnp.logical_or(filled, block >= me)
        for r in range(0, rows, sub):
            t = slice(r // group, (r + sub) // group)
            qf = q_ref[t, :, :].astype(jnp.float32)
            qf = qf[:, h * group : (h + 1) * group, :].reshape(sub, hd) * scale
            high = qf.astype(jnp.bfloat16)
            low = (qf - high.astype(jnp.float32)).astype(jnp.bfloat16)
            q2 = jnp.concatenate([high, low], axis=1)
            s = lax.dot_general(
                q2, k_s[h], (((1,), (1,)), ((), ())), preferred_element_type=jnp.float32
            )
            s_new = jnp.where(dist[r : r + sub, :] >= least, s[:, slots:], NEG)
            s_old = s[:, :slots]
            peak = jnp.maximum(
                jnp.max(s_old, axis=1, keepdims=True), jnp.max(s_new, axis=1, keepdims=True)
            )
            p_old = jnp.exp2(s_old - peak).astype(jnp.bfloat16)
            p_new = jnp.exp2(s_new - peak).astype(jnp.bfloat16)
            o = jnp.dot(p_old, v_s[h, :slots, :], preferred_element_type=jnp.float32)
            o = o + jnp.dot(p_new, v_s[h, slots:, :], preferred_element_type=jnp.float32)
            total = jnp.maximum(o[:, hd:], 1.0)
            norm = o[:, :hd] / total
            lse = jnp.where(some, peak + jnp.log2(total), NEG)
            emit(r, norm, lse)

    def keep(o_ref, l_ref):
        def emit(r, norm, lse):
            o_ref[r : r + sub, :] = norm
            l_ref[r : r + sub, :] = lse
        return emit

    def ship(o_ref, l_ref):
        def emit(r, norm, lse):
            o_ref[r : r + sub, :] = norm.astype(jnp.bfloat16)
            for i, row in enumerate(column_to_rows(lse)):
                l_ref[r // 128 + i : r // 128 + i + 1, :] = row
        return emit

    def start(pair):
        pair[0].start()
        pair[1].start()

    def merge(o_ref, l_ref, parts, r):
        outs = [o_ref[r : r + 128, :]]
        lses = [l_ref[r : r + 128, :]]
        for po, pl_ in parts:
            outs.append(po[r : r + 128, :].astype(jnp.float32))
            lses.append(rows_to_column(pl_[r // 128 : r // 128 + 1, :]))
        top = functools.reduce(jnp.maximum, lses)
        weights = [jnp.exp2(l - top) for l in lses]
        den = functools.reduce(jnp.add, weights)
        num = functools.reduce(jnp.add, [w * o for w, o in zip(weights, outs)])
        return num / den, top + jnp.log2(den)

    loads[2].wait()
    send_q_part.wait_recv()
    for h in range(nh):
        attend(q_part, h, partner, ship(sp_o.at[h], sp_l.at[h]))
        start(send_pp[h])
    for h in range(nh - 1):
        attend(q_own, h, me, keep(own_o.at[h], own_l.at[h]))

    for d in range(chips - 1):
        send_q_far[d].wait_recv()
        send_q_rel[d].start()
        a_block = back[d]
        b_block = a_block + 1 - 2 * core

        def join(h, d=d):
            send_pb[d][h][0].wait_recv()
            send_pb[d][h][1].wait_recv()
            for r in range(0, rows, 128):
                norm, lse = merge(
                    a_o.at[h], a_l.at[h], [(pb_o.at[d, h], pb_l.at[d, h])], r
                )
                sr_o[d, h, r : r + 128, :] = norm.astype(jnp.bfloat16)
                sr_l[d, h, r // 128 : r // 128 + 1, :] = column_to_rows(lse)[0]
            start(send_pr[d][h])

        attend(q_rem.at[d], 0, a_block, keep(a_o.at[0], a_l.at[0]))
        send_q_rel[d].wait_recv()
        for h in range(nh):
            attend(q_rel.at[d], h, b_block, ship(sb_o.at[d, h], sb_l.at[d, h]))
            start(send_pb[d][h])
        join(0)
        for h in range(1, nh):
            attend(q_rem.at[d], h, a_block, keep(a_o.at[h], a_l.at[h]))
            join(h)

    attend(q_own, nh - 1, me, keep(own_o.at[nh - 1], own_l.at[nh - 1]))

    for h in range(nh):
        send_pp[h][0].wait_recv()
        send_pp[h][1].wait_recv()
    for d in range(chips - 1):
        for h in range(nh):
            send_pr[d][h][0].wait_recv()
            send_pr[d][h][1].wait_recv()
    for r in range(0, rows, 128):
        pieces = []
        for h in range(nh):
            parts = [(pp_o.at[h], pp_l.at[h])]
            parts += [(pr_o.at[d, h], pr_l.at[d, h]) for d in range(chips - 1)]
            norm, _ = merge(own_o.at[h], own_l.at[h], parts, r)
            pieces.append(norm.reshape(128 // group, group, hd))
        full = jnp.concatenate(pieces, axis=1) if nh > 1 else pieces[0]
        out_ref[r // group : (r + 128) // group, :, :] = full.astype(jnp.bfloat16)

    for c in send_q_far + [send_q_part] + send_q_rel:
        c.wait_send()
    for pair in send_pp + [p for ps in send_pb for p in ps] + [p for ps in send_pr for p in ps]:
        pair[0].wait_send()
        pair[1].wait_send()


def per_device(n_ctx, queries, new_keys, new_values, cache_keys, cache_values, cache_len):
    tokens, heads, hd = queries.shape
    slots, nh, _ = cache_keys.shape
    group = heads // nh
    rows = tokens * group
    chips = n_ctx // 2
    far = chips - 1
    ext = -(-tokens // 128) * 128
    f32, bf16 = jnp.float32, jnp.bfloat16
    lr = rows // 128
    n_copies = far + 1 + far + 2 * nh + 4 * far * nh
    flat = lambda x: x.reshape(x.shape[0] * nh, hd)
    vmem, hbm = pl.BlockSpec(memory_space=pltpu.VMEM), pl.BlockSpec(memory_space=pl.ANY)
    return pl.pallas_call(
        functools.partial(kernel, chips, nh, group, min(256, rows)),
        out_shape=jax.ShapeDtypeStruct(queries.shape, bf16),
        in_specs=[pl.BlockSpec(memory_space=pltpu.SMEM), hbm, vmem, vmem, hbm, hbm],
        out_specs=vmem,
        scratch_shapes=[
            pltpu.VMEM((slots * nh, hd), bf16),
            pltpu.VMEM((slots * nh, hd), bf16),
            pltpu.VMEM((2, CHUNK * nh, hd), f32),
            pltpu.VMEM((nh, slots + ext, 2 * hd), bf16),
            pltpu.VMEM((nh, slots + ext, 2 * hd), bf16),
            pltpu.VMEM((rows, ext), jnp.int32),
            pltpu.VMEM(queries.shape, bf16),
            pltpu.VMEM(queries.shape, bf16),
            pltpu.VMEM((far,) + queries.shape, bf16),
            pltpu.VMEM((far,) + queries.shape, bf16),
            pltpu.VMEM((nh, rows, hd), f32),
            pltpu.VMEM((nh, rows, hd), f32),
            pltpu.VMEM((nh, rows, hd), f32),
            pltpu.VMEM((nh, rows, hd), f32),
            pltpu.VMEM((nh, rows, hd), bf16),
            pltpu.VMEM((nh, lr, 128), f32),
            pltpu.VMEM((far, nh, rows, hd), bf16),
            pltpu.VMEM((far, nh, lr, 128), f32),
            pltpu.VMEM((far, nh, rows, hd), bf16),
            pltpu.VMEM((far, nh, lr, 128), f32),
            pltpu.VMEM((nh, rows, hd), bf16),
            pltpu.VMEM((nh, lr, 128), f32),
            pltpu.VMEM((far, nh, rows, hd), bf16),
            pltpu.VMEM((far, nh, lr, 128), f32),
            pltpu.VMEM((far, nh, rows, hd), bf16),
            pltpu.VMEM((far, nh, lr, 128), f32),
            pltpu.SemaphoreType.DMA((3,)),
            pltpu.SemaphoreType.DMA((n_copies,)),
            pltpu.SemaphoreType.DMA((n_copies,)),
        ],
        compiler_params=pltpu.CompilerParams(
            collective_id=0, has_side_effects=True, vmem_limit_bytes=60 * 1024 * 1024
        ),
        name="turn_attention",
    )(cache_len, queries, flat(new_keys), flat(new_values), flat(cache_keys), flat(cache_values))


def solution(mesh):
    split = P(("conv", "ctx"), "head", None)
    return jax.shard_map(
        functools.partial(per_device, mesh.shape["ctx"]),
        mesh=mesh,
        in_specs=(split, split, split, split, split, P("conv")),
        out_specs=split,
        check_vma=False,
    )
```

time: 125 us -> 30.9 us (0.25)
  matrix products: 33.2 us -> 0 us
  Pallas kernels: 0 us -> 28.3 us
  local copies, waits for them, and re-layouts: 23.8 us -> 1.67 us
  waiting for transfers between devices: 19.2 us -> 0 us
  other arithmetic: 14.9 us -> 0 us
  between operations: 13.5 us -> 0.66 us
  blocking collectives: 12.8 us -> 0 us
  starting transfers between devices: 6.77 us -> 0 us
    dot_general x11 -> x0, matrix products: 33.2 us -> none  [the longest x5 20.8 us: attend_block(): jnp.einsum('tkgs,skd->tkgd', expo.astype(jnp.bfloat16), values, preferred...]
    pallas_call x0 -> x1, Pallas kernels: none -> 28.3 us  [per_device(): pl.pallas_call(functools.partial(kernel, chips, nh, group, min(256, rows)...]
    all_to_all x2 -> x0, waiting for transfers between devices: 15.7 us -> none  [the longest x1 12.2 us: per_device(): lax.all_to_all(norm[None], 'ctx', split_axis=1, concat_axis=0, tiled=True)]
    while x8 -> x0, local copies, waits for them, and re-layouts: 12.9 us -> none
    all_gather x2 -> x0, blocking collectives: 12.8 us -> none  [the longest x1 6.49 us: per_device(): lax.all_gather(new_keys, 'ctx', axis=0, tiled=True)]
    reduce_sum x6 -> x0, other arithmetic: 9.32 us -> none  [the longest x5 9.28 us: attend_block(): total = jnp.sum(expo, axis=-1)]
    all_to_all x2 -> x0, starting transfers between devices: 6.77 us -> none  [the longest x1 3.52 us: per_device(): lax.all_to_all(norm[None], 'ctx', split_axis=1, concat_axis=0, tiled=True)]
    unnamed x7 -> x1, local copies, waits for them, and re-layouts: 5.81 us -> 1.67 us
  transfers between devices with their start and end apart: 3 -> 0, of which waited for: 3 -> 0; matrix products, arithmetic and copies ran while one was open for 7% -> 0% of each run, Pallas kernels for 0% -> 0%
where the time goes in v1:
time: 30.9 us; the launch traced here: 30.7 us
  Pallas kernels  28.3 us (92%)
  local copies, waits for them, and re-layouts  1.67 us (5%)
  between operations  0.66 us (2%)
    pallas_call x1, Pallas kernels, per_device(): pl.pallas_call(functools.partial(kernel, chips, nh, group, min(256, rows)...  28.3 us
    unnamed x1, local copies, waits for them, and re-layouts  1.67 us

profile of v1, /device:TPU:0, one launch (start us, length us, event | category | flops | bytes accessed | tf_op | source)
XLA Modules:
  0.0 30.7 jit_solution(13093974574869431095)
XLA Ops:
  0.7 28.3 %turn_attention.1 = bf16[64,16,128]{2,1,0:T(8,128)(2,1)} custom-call(s32[1]{0:T(128)S(6)} %copy.8.len_ref, bf16[64,16,128]{2,1,0:T(8,128)(2,1)} %q_hbm.1, bf16[128,128]{1,0:T(8,128)(2,1)} %bitcast.6, bf16[128,128]{1,0:T(8,128)(2,1)} %bitcast.7, bf16[4096,128]{1,0:T(8,128)(2,1)} %bitcast.4, bf16[4096,128]{1,0:T(8,128)(2,1)} %bitcast.5), custom_call_target="tpu_custom_call" | custom-call | tf_op jit(solution)/shard_map/turn_attention/pallas_call | solution.py:276
  29.0 1.7 %copy.9 = bf16[64,16,128]{2,1,0:T(8,128)(2,1)} copy(bf16[64,16,128]{2,1,0:T(8,128)(2,1)} %turn_attention.1) | data formatting | bytes 524288
